TPU v7x, 32 devices: a whole 2x2x4 slice. The times are simulated.
32 devices in a mesh: design: 2 (over x), domain: 16 (over z, y, core).
Axes of the slice: x: 2, y: 2, z: 4, core: 2. Of those that a mesh axis runs over, the one named last changes fastest.
Arguments:
- e_field: float32 [3, 128, 64, 128], P(None, ('design', 'domain')), parts along dimension 1, may hold values from -6 to 6
- h_field: float32 [3, 128, 64, 128], P(None, ('design', 'domain')), parts along dimension 1, may hold values from -6 to 6
- adj_e_field: float32 [3, 128, 64, 128], P(None, ('design', 'domain')), parts along dimension 1, may hold values from -6 to 6
- adj_h_field: float32 [3, 128, 64, 128], P(None, ('design', 'domain')), parts along dimension 1, may hold values from -6 to 6
- permittivity: float32 [3, 256], P(None, ('design', 'domain')), parts along dimension 1, may hold values from 1 to 6
- conductivity: float32 [3, 256], P(None, ('design', 'domain')), parts along dimension 1, may hold values from 0.02 to 0.6
- region_labels: int32 [128, 8, 16], P(('design', 'domain')), parts along dimension 0, may hold values from 0 to 127
- source_plane: int32 [2], P('design'), parts along dimension 0, may hold values from 0 to 63
- monitor_plane: int32 [2], P('design'), parts along dimension 0, may hold values from 0 to 63
- wave_index: int32 [8], P('design'), parts along dimension 0, may hold values from 0 to 15
- source_mode: float32 [128, 128], P('design'), parts along dimension 0, may hold values from -6 to 6
- monitor_mode: float32 [128, 128], P('design'), parts along dimension 0, may hold values from -6 to 6
Outputs:
- region_grads: float32 [6, 256], P(None, ('design', 'domain')), parts along dimension 1
There are 2 independent parts, one for each index of `design`. A program takes and returns all parts, laid end to end along the dimension named above; each array names one. Nothing has to cross between parts.
All inputs are finite; a program needn't handle non-finite values.
Results may differ from a plain program's by a relative error of at most 0.0003.
Values sent between devices are 32-bit elements; how exact they have to be, the bound alone decides.
A program may use at most 64 MiB of HBM per device.

v0:
```python
import math

import jax
import jax.numpy as jnp
from jax import lax
from jax.sharding import PartitionSpec as P

STEPS = 8
NF = 4


COURANT = 0.5


def from_behind(x, axis, by):
    count = lax.axis_size(axis)
    pairs = [(i, i + by) for i in range(count) if 0 <= i + by < count]
    return lax.ppermute(x, axis, pairs)


def lagged(values, axis):
    zero = jnp.zeros_like(lax.slice_in_dim(values, 0, 1, axis=axis))
    return jnp.concatenate(
        [zero, lax.slice_in_dim(values, 0, values.shape[axis] - 1, axis=axis)], axis=axis
    )


def leading(values, axis):
    zero = jnp.zeros_like(lax.slice_in_dim(values, 0, 1, axis=axis))
    return jnp.concatenate(
        [lax.slice_in_dim(values, 1, values.shape[axis], axis=axis), zero], axis=axis
    )


def new_electric(electric, magnetic, hy_left, hz_left, keep_rate, gain_rate, forcing, component):
    curl_x = magnetic[2] - lagged(magnetic[2], 1) - (magnetic[1] - lagged(magnetic[1], 2))
    curl_y = magnetic[0] - lagged(magnetic[0], 2) - (magnetic[2] - hz_left)
    curl_z = magnetic[1] - hy_left - (magnetic[0] - lagged(magnetic[0], 1))
    curls = (curl_x, curl_y, curl_z)
    updated = []
    for c in range(3):
        pushing = COURANT * curls[c]
        if c == component:
            pushing = pushing - forcing
        updated.append(keep_rate[c] * electric[c] + gain_rate[c] * pushing)
    return jnp.stack(updated)


def new_magnetic(magnetic, electric, ey_right, ez_right):
    curl_x = leading(electric[2], 1) - electric[2] - (leading(electric[1], 2) - electric[1])
    curl_y = leading(electric[0], 2) - electric[0] - (ez_right - electric[2])
    curl_z = ey_right - electric[1] - (leading(electric[0], 1) - electric[0])
    return jnp.stack(
        [
            magnetic[0] - COURANT * curl_x,
            magnetic[1] - COURANT * curl_y,
            magnetic[2] - COURANT * curl_z,
        ]
    )


def spread(blocks):
    shape = blocks.shape
    grown = jnp.broadcast_to(
        blocks[:, :, :, None, :, None], (shape[0], shape[1], shape[2], 8, shape[3], 8)
    )
    return grown.reshape(shape[0], shape[1], shape[2] * 8, shape[3] * 8)


def plane_profile(plane, shape_mode, count, width):
    layers = lax.axis_index("domain") * width + jnp.arange(count, dtype=jnp.int32)
    return jnp.where(layers[:, None, None] == plane, shape_mode[None], 0.0)


def accumulate(spectra_re, spectra_im, cosines, sines, electric):
    spectra_re = spectra_re + cosines[:, None, None, None, None] * electric[None]
    spectra_im = spectra_im - sines[:, None, None, None, None] * electric[None]
    return (spectra_re, spectra_im)


def evolve(electric, magnetic, rates, plane, shape_mode, component, amp_cos, amp_sin, omega):
    width = electric.shape[1]
    spectra_re = jnp.zeros((omega.shape[0],) + electric.shape, jnp.float32)
    spectra_im = jnp.zeros((omega.shape[0],) + electric.shape, jnp.float32)
    keep_rate, gain_rate = rates
    profile = plane_profile(plane, shape_mode, width, width)
    for step in range(STEPS):
        moment = jnp.float32(step + 1)
        cosines = jnp.cos(omega * moment)
        sines = jnp.sin(omega * moment)
        forcing = profile * jnp.sum(amp_cos * cosines + amp_sin * sines)
        incoming = from_behind(jnp.stack([magnetic[1, -1:], magnetic[2, -1:]]), "domain", 1)
        hy_left = jnp.concatenate([incoming[0], magnetic[1, :-1]], 0)
        hz_left = jnp.concatenate([incoming[1], magnetic[2, :-1]], 0)
        electric = new_electric(
            electric, magnetic, hy_left, hz_left, keep_rate, gain_rate, forcing, component
        )
        outgoing = from_behind(jnp.stack([electric[1, :1], electric[2, :1]]), "domain", -1)
        ey_right = jnp.concatenate([electric[1, 1:], outgoing[0]], 0)
        ez_right = jnp.concatenate([electric[2, 1:], outgoing[1]], 0)
        magnetic = new_magnetic(magnetic, electric, ey_right, ez_right)
        spectra_re, spectra_im = accumulate(spectra_re, spectra_im, cosines, sines, electric)
    return (spectra_re, spectra_im)


def local(
    e_field,
    h_field,
    adj_e_field,
    adj_h_field,
    permittivity,
    conductivity,
    region_labels,
    source_plane,
    monitor_plane,
    wave_index,
    source_mode,
    monitor_mode,
):
    width = e_field.shape[1]
    rows_y = e_field.shape[2]
    rows_z = e_field.shape[3]
    per_device = permittivity.shape[1]
    omega = 0.25 + 0.05 * wave_index.astype(jnp.float32)
    perm_all, cond_all = (
        lax.all_gather(permittivity, "domain", axis=1, tiled=True),
        lax.all_gather(conductivity, "domain", axis=1, tiled=True),
    )
    regions = perm_all.shape[1]
    flat_labels = region_labels.reshape(-1)
    selector = (jnp.arange(regions, dtype=jnp.int32)[:, None] == flat_labels[None, :]).astype(
        jnp.float32
    )
    block_shape = (3,) + region_labels.shape
    perm_blocks = jnp.dot(perm_all, selector, precision=lax.Precision.HIGHEST).reshape(block_shape)
    cond_blocks = jnp.dot(cond_all, selector, precision=lax.Precision.HIGHEST).reshape(block_shape)
    loss = cond_blocks * 0.5 / perm_blocks
    keep_rate = spread((1.0 - loss) / (1.0 + loss))
    gain_rate = spread(1.0 / (perm_blocks * (1.0 + loss)))
    rates = (keep_rate, gain_rate)
    zeros_amp = jnp.zeros((NF,), jnp.float32)
    ones_amp = jnp.ones((NF,), jnp.float32)
    fwd_re, fwd_im = evolve(
        e_field, h_field, rates, source_plane[0], source_mode, 2, zeros_amp, ones_amp, omega
    )
    rank = lax.axis_index("domain")
    root = math.sqrt(rows_y * rows_z)
    local_mon = monitor_plane[0] - rank * width
    holds_mon = ((local_mon >= 0) & (local_mon < width)).astype(jnp.float32)
    mon_index = jnp.clip(local_mon, 0, width - 1)
    mon_re = lax.dynamic_slice_in_dim(fwd_re[:, 1], mon_index, 1, 1)[:, 0]
    mon_im = lax.dynamic_slice_in_dim(fwd_im[:, 1], mon_index, 1, 1)[:, 0]
    local_src = source_plane[0] - rank * width
    holds_src = ((local_src >= 0) & (local_src < width)).astype(jnp.float32)
    src_index = jnp.clip(local_src, 0, width - 1)
    src_re = lax.dynamic_slice_in_dim(fwd_re[:, 2], src_index, 1, 1)[:, 0]
    src_im = lax.dynamic_slice_in_dim(fwd_im[:, 2], src_index, 1, 1)[:, 0]
    intersection_re = jnp.sum(mon_re * monitor_mode, axis=(1, 2)) / root * holds_mon
    intersection_im = jnp.sum(mon_im * monitor_mode, axis=(1, 2)) / root * holds_mon
    power = jnp.mean(src_re * src_re + src_im * src_im, axis=(1, 2)) * holds_src
    intersection_re, intersection_im, power = lax.psum(
        (intersection_re, intersection_im, power), "domain"
    )
    scale = 1.0 / jnp.sqrt(power + 1e-06)
    adj_re, adj_im = evolve(
        adj_e_field,
        adj_h_field,
        rates,
        monitor_plane[0],
        monitor_mode,
        1,
        intersection_re * scale,
        intersection_im * scale,
        omega,
    )
    squared = omega * omega
    grad_perm = jnp.sum(
        squared[:, None, None, None, None] * (fwd_re * adj_re - fwd_im * adj_im), axis=0
    )
    grad_cond = jnp.sum(
        omega[:, None, None, None, None] * (fwd_re * adj_im + fwd_im * adj_re), axis=0
    )
    cellwise = jnp.concatenate([grad_perm, grad_cond], 0)
    blocks = (
        cellwise.reshape(6, width, rows_y // 8, 8, rows_z // 8, 8).sum(axis=(3, 5)).reshape(6, -1)
    )
    partial_grads = jnp.einsum("cb,rb->cr", blocks, selector, precision=lax.Precision.HIGHEST)
    summed = lax.psum(partial_grads, "domain")
    owned_grads = lax.dynamic_slice_in_dim(summed, rank * per_device, per_device, 1)
    total_cells = lax.axis_size("domain") * width * rows_y * rows_z
    return owned_grads * math.sqrt(regions / total_cells)


def solution(mesh):
    placed = (
        P(None, ("design", "domain"), None, None),
        P(None, ("design", "domain"), None, None),
        P(None, ("design", "domain"), None, None),
        P(None, ("design", "domain"), None, None),
        P(None, ("design", "domain")),
        P(None, ("design", "domain")),
        P(("design", "domain"), None, None),
        P("design"),
        P("design"),
        P("design"),
        P("design", None),
        P("design", None),
    )
    return jax.shard_map(
        local, mesh=mesh, in_specs=placed, out_specs=P(None, ("design", "domain")), check_vma=False
    )
```

profile of v0, /device:TPU:0, one launch (start us, length us, event | category | flops | bytes accessed | tf_op | source)
XLA Modules:
  0.0 319.9 jit_solution(11958374379330959637)
XLA Ops:
  1.5 3.0 collective-permute-start.15
  6.0 4.6 %collective-permute-start = (f32[2,1,64,128]{3,2,1,0:T(8,128)}, f32[2,1,64,128]{3,2,1,0:T(8,128)}, u32[]{:S(2)}, u32[]{:S(2)}) collective-permute-start(f32[2,1,64,128]{3,2,1,0:T(8,128)} %stack.367), channel_id=1, source_target_pairs={{0,1},{1,2},{2,3},{3,4},{4,5},{5,6},{6,7},{7,8},{8,9},{9,10},{10,1... | collective-permute-start | bytes 196616 | tf_op jit(solution)/shard_map/ppermute | solution.py:18
  19.1 19.5 %all-gather.1 = f32[16,8,3]{1,2,0:T(4,128)S(1)} all-gather(f32[1,8,3]{1,2,0:T(4,128)S(1)} %bitcast.735), channel_id=1, replica_groups=mesh['design'=2,'domain'=16] {'domain'}, dimensions={0}, use_global_device_ids=true | all-gather | bytes 1632 | tf_op jit(solution)/shard_map/all_gather | solution.py:126
  38.7 17.5 %all-gather = f32[16,8,3]{1,2,0:T(4,128)S(1)} all-gather(f32[1,8,3]{1,2,0:T(4,128)S(1)} %bitcast.736), channel_id=1, replica_groups=mesh['design'=2,'domain'=16] {'domain'}, dimensions={0}, use_global_device_ids=true | all-gather | bytes 1632 | tf_op jit(solution)/shard_map/all_gather | solution.py:127
  74.6 4.7 %collective-permute-start.2 = (f32[2,1,64,128]{3,2,1,0:T(8,128)S(1)}, f32[2,1,64,128]{3,2,1,0:T(8,128)S(1)}, u32[]{:S(2)}, u32[]{:S(2)}) collective-permute-start(f32[2,1,64,128]{3,2,1,0:T(8,128)S(1)} %pad_maximum_fusion.18), channel_id=1, source_target_pairs={{0,1},{1,2},{2,3},{3,4},{4,5},{5,6},{6,7},{7,8},{8,9},{9,10},{10,1... | collective-permute-start | bytes 196616 | tf_op jit(solution)/shard_map/ppermute | solution.py:18
  84.7 5.4 %collective-permute-start.4 = (f32[2,1,64,128]{3,2,1,0:T(8,128)S(1)}, f32[2,1,64,128]{3,2,1,0:T(8,128)S(1)}, u32[]{:S(2)}, u32[]{:S(2)}) collective-permute-start(f32[2,1,64,128]{3,2,1,0:T(8,128)S(1)} %pad_maximum_fusion.20), channel_id=1, source_target_pairs={{0,1},{1,2},{2,3},{3,4},{4,5},{5,6},{6,7},{7,8},{8,9},{9,10},{10,1... | collective-permute-start | bytes 196616 | tf_op jit(solution)/shard_map/ppermute | solution.py:18
  95.6 6.4 %collective-permute-start.6 = (f32[2,1,64,128]{3,2,1,0:T(8,128)S(1)}, f32[2,1,64,128]{3,2,1,0:T(8,128)S(1)}, u32[]{:S(2)}, u32[]{:S(2)}) collective-permute-start(f32[2,1,64,128]{3,2,1,0:T(8,128)S(1)} %pad_maximum_fusion.22), channel_id=1, source_target_pairs={{0,1},{1,2},{2,3},{3,4},{4,5},{5,6},{6,7},{7,8},{8,9},{9,10},{10,1... | collective-permute-start | bytes 196616 | tf_op jit(solution)/shard_map/ppermute | solution.py:18
  107.2 6.3 %collective-permute-start.8 = (f32[2,1,64,128]{3,2,1,0:T(8,128)S(1)}, f32[2,1,64,128]{3,2,1,0:T(8,128)S(1)}, u32[]{:S(2)}, u32[]{:S(2)}) collective-permute-start(f32[2,1,64,128]{3,2,1,0:T(8,128)S(1)} %pad_maximum_fusion.24), channel_id=1, source_target_pairs={{0,1},{1,2},{2,3},{3,4},{4,5},{5,6},{6,7},{7,8},{8,9},{9,10},{10,1... | collective-permute-start | bytes 196616 | tf_op jit(solution)/shard_map/ppermute | solution.py:18
  118.9 6.3 %collective-permute-start.10 = (f32[2,1,64,128]{3,2,1,0:T(8,128)S(1)}, f32[2,1,64,128]{3,2,1,0:T(8,128)S(1)}, u32[]{:S(2)}, u32[]{:S(2)}) collective-permute-start(f32[2,1,64,128]{3,2,1,0:T(8,128)S(1)} %pad_maximum_fusion.26), channel_id=1, source_target_pairs={{0,1},{1,2},{2,3},{3,4},{4,5},{5,6},{6,7},{7,8},{8,9},{9,10},{10,1... | collective-permute-start | bytes 196616 | tf_op jit(solution)/shard_map/ppermute | solution.py:18
  130.6 6.3 %collective-permute-start.12 = (f32[2,1,64,128]{3,2,1,0:T(8,128)S(1)}, f32[2,1,64,128]{3,2,1,0:T(8,128)S(1)}, u32[]{:S(2)}, u32[]{:S(2)}) collective-permute-start(f32[2,1,64,128]{3,2,1,0:T(8,128)S(1)} %pad_maximum_fusion.28), channel_id=1, source_target_pairs={{0,1},{1,2},{2,3},{3,4},{4,5},{5,6},{6,7},{7,8},{8,9},{9,10},{10,1... | collective-permute-start | bytes 196616 | tf_op jit(solution)/shard_map/ppermute | solution.py:18
  142.4 6.3 %collective-permute-start.14 = (f32[2,1,64,128]{3,2,1,0:T(8,128)S(1)}, f32[2,1,64,128]{3,2,1,0:T(8,128)S(1)}, u32[]{:S(2)}, u32[]{:S(2)}) collective-permute-start(f32[2,1,64,128]{3,2,1,0:T(8,128)S(1)} %pad_maximum_fusion.30), channel_id=1, source_target_pairs={{0,1},{1,2},{2,3},{3,4},{4,5},{5,6},{6,7},{7,8},{8,9},{9,10},{10,1... | collective-permute-start | bytes 196616 | tf_op jit(solution)/shard_map/ppermute | solution.py:18
  157.5 30.6 %all-reduce.120 = (f32[4]{0:T(128)}, f32[4]{0:T(128)}, f32[4]{0:T(128)}) all-reduce(f32[4]{0:T(128)} %broadcast_multiply_fusion.1, f32[4]{0:T(128)} %broadcast_multiply_fusion, f32[4]{0:T(128)} %broadcast_multiply_fusion.2), channel_id=1, replica_groups=mesh['design'=2,'domain'=16] {'domain'}, use_global_device_ids=true, to_apply=%region_13.14 | all-reduce | flops 12 | bytes 96 | tf_op jit(solution)/shard_map/psum | solution.py:161
  195.9 3.8 %collective-permute-start.17 = (f32[2,1,64,128]{3,2,1,0:T(8,128)S(1)}, f32[2,1,64,128]{3,2,1,0:T(8,128)S(1)}, u32[]{:S(2)}, u32[]{:S(2)}) collective-permute-start(f32[2,1,64,128]{3,2,1,0:T(8,128)S(1)} %pad_maximum_fusion.32), channel_id=1, source_target_pairs={{0,1},{1,2},{2,3},{3,4},{4,5},{5,6},{6,7},{7,8},{8,9},{9,10},{10,1... | collective-permute-start | bytes 196616 | tf_op jit(solution)/shard_map/ppermute | solution.py:18
  205.0 5.4 %collective-permute-start.19 = (f32[2,1,64,128]{3,2,1,0:T(8,128)S(1)}, f32[2,1,64,128]{3,2,1,0:T(8,128)S(1)}, u32[]{:S(2)}, u32[]{:S(2)}) collective-permute-start(f32[2,1,64,128]{3,2,1,0:T(8,128)S(1)} %pad_maximum_fusion.34), channel_id=1, source_target_pairs={{0,1},{1,2},{2,3},{3,4},{4,5},{5,6},{6,7},{7,8},{8,9},{9,10},{10,1... | collective-permute-start | bytes 196616 | tf_op jit(solution)/shard_map/ppermute | solution.py:18
  215.9 5.4 %collective-permute-start.21 = (f32[2,1,64,128]{3,2,1,0:T(8,128)S(1)}, f32[2,1,64,128]{3,2,1,0:T(8,128)S(1)}, u32[]{:S(2)}, u32[]{:S(2)}) collective-permute-start(f32[2,1,64,128]{3,2,1,0:T(8,128)S(1)} %pad_maximum_fusion.36), channel_id=1, source_target_pairs={{0,1},{1,2},{2,3},{3,4},{4,5},{5,6},{6,7},{7,8},{8,9},{9,10},{10,1... | collective-permute-start | bytes 196616 | tf_op jit(solution)/shard_map/ppermute | solution.py:18
  226.7 5.4 %collective-permute-start.23 = (f32[2,1,64,128]{3,2,1,0:T(8,128)S(1)}, f32[2,1,64,128]{3,2,1,0:T(8,128)S(1)}, u32[]{:S(2)}, u32[]{:S(2)}) collective-permute-start(f32[2,1,64,128]{3,2,1,0:T(8,128)S(1)} %pad_maximum_fusion.38), channel_id=1, source_target_pairs={{0,1},{1,2},{2,3},{3,4},{4,5},{5,6},{6,7},{7,8},{8,9},{9,10},{10,1... | collective-permute-start | bytes 196616 | tf_op jit(solution)/shard_map/ppermute | solution.py:18
  237.4 5.4 %collective-permute-start.25 = (f32[2,1,64,128]{3,2,1,0:T(8,128)S(1)}, f32[2,1,64,128]{3,2,1,0:T(8,128)S(1)}, u32[]{:S(2)}, u32[]{:S(2)}) collective-permute-start(f32[2,1,64,128]{3,2,1,0:T(8,128)S(1)} %pad_maximum_fusion.40), channel_id=1, source_target_pairs={{0,1},{1,2},{2,3},{3,4},{4,5},{5,6},{6,7},{7,8},{8,9},{9,10},{10,1... | collective-permute-start | bytes 196616 | tf_op jit(solution)/shard_map/ppermute | solution.py:18
  248.2 5.5 %collective-permute-start.27 = (f32[2,1,64,128]{3,2,1,0:T(8,128)S(1)}, f32[2,1,64,128]{3,2,1,0:T(8,128)S(1)}, u32[]{:S(2)}, u32[]{:S(2)}) collective-permute-start(f32[2,1,64,128]{3,2,1,0:T(8,128)S(1)} %pad_maximum_fusion.42), channel_id=1, source_target_pairs={{0,1},{1,2},{2,3},{3,4},{4,5},{5,6},{6,7},{7,8},{8,9},{9,10},{10,1... | collective-permute-start | bytes 196616 | tf_op jit(solution)/shard_map/ppermute | solution.py:18
  259.1 6.5 %collective-permute-start.29 = (f32[2,1,64,128]{3,2,1,0:T(8,128)S(1)}, f32[2,1,64,128]{3,2,1,0:T(8,128)S(1)}, u32[]{:S(2)}, u32[]{:S(2)}) collective-permute-start(f32[2,1,64,128]{3,2,1,0:T(8,128)S(1)} %pad_maximum_fusion.44), channel_id=1, source_target_pairs={{0,1},{1,2},{2,3},{3,4},{4,5},{5,6},{6,7},{7,8},{8,9},{9,10},{10,1... | collective-permute-start | bytes 196616 | tf_op jit(solution)/shard_map/ppermute | solution.py:18
  267.6 3.5 %multiply_reduce_fusion = f32[3,4,64,128]{3,2,1,0:T(8,128)S(1)} fusion(f32[4]{0:T(128)S(1)} %copy-done.61, f32[3,4,64,128]{3,2,1,0:T(8,128)S(1)} %pad_maximum_fusion.16, f32[3,4,64,128]{3,2,1,0:T(8,128)S(1)} %pad_maximum_fusion.15, f32[3,4,64,128]{3,2,1,0:T(8,128)S(1)} %pad_maximum_fusion.14, f32[3,4,64,128]{3,2,1,0:T(8,128)S(1)} %pad_maximum_fusion.13, ...), kind=kLoop, calls=%fused_computation | loop fusion | flops 26247168 | bytes 6684944 | tf_op jit(solution)/shard_map/reduce_sum | solution.py:180
  271.1 3.5 %multiply_reduce_fusion.1 = f32[3,4,64,128]{3,2,1,0:T(8,128)S(1)} fusion(f32[3,4,64,128]{3,2,1,0:T(8,128)S(1)} %pad_maximum_fusion.16, f32[3,4,64,128]{3,2,1,0:T(8,128)S(1)} %pad_maximum_fusion.15, f32[3,4,64,128]{3,2,1,0:T(8,128)S(1)} %pad_maximum_fusion.14, f32[3,4,64,128]{3,2,1,0:T(8,128)S(1)} %pad_maximum_fusion.13, ...), kind=kLoop, calls=%fused_computation.1 | loop fusion | flops 26247168 | bytes 6684944 | tf_op jit(solution)/shard_map/reduce_sum | solution.py:177
  274.8 8.8 %reshape.158 = f32[6,4,8,8,16,8]{5,4,3,2,1,0:T(8,128)} reshape(f32[6,4,64,128]{3,2,1,0:T(8,128)S(1)} %pad_maximum_fusion) | data formatting | bytes 1572864 | tf_op jit(solution)/shard_map/reshape | solution.py:185
  283.5 5.5 %reduce_sum.219 = f32[6,4,8,16]{3,2,1,0:T(8,128)S(1)} reduce(f32[6,4,8,8,16,8]{5,4,3,2,1,0:T(8,128)} %reshape.158, f32[]{:T(128)} %constant.26.clone.1), dimensions={3,5}, to_apply=%region_24.25 | reduce | flops 193536 | bytes 798724 | tf_op jit(solution)/shard_map/reduce_sum | solution.py:185
  289.3 30.0 %psum.31 = f32[6,128]{1,0:T(8,128)S(1)} all-reduce(f32[6,128]{1,0:T(8,128)S(1)} %fusion.1), channel_id=1, replica_groups=mesh['design'=2,'domain'=16] {'domain'}, use_global_device_ids=true, to_apply=%region_25.26 | all-reduce | flops 768 | bytes 6144 | tf_op jit(solution)/shard_map/psum | solution.py:188
  (503 shorter events, 110.1 us)
Async XLA Ops:
  1.5 65.0 %collective-permute-start.15 = (f32[2,1,64,128]{3,2,1,0:T(8,128)}, f32[2,1,64,128]{3,2,1,0:T(8,128)}, u32[]{:S(2)}, u32[]{:S(2)}) collective-permute-start(f32[2,1,64,128]{3,2,1,0:T(8,128)} %stack.428), channel_id=1, source_target_pairs={{0,1},{1,2},{2,3},{3,4},{4,5},{5,6},{6,7},{7,8},{8,9},{9,10},{10,1... | collective-permute-start | bytes 196616 | tf_op jit(solution)/shard_map/ppermute | solution.py:18
  6.0 58.5 %collective-permute-start = (f32[2,1,64,128]{3,2,1,0:T(8,128)}, f32[2,1,64,128]{3,2,1,0:T(8,128)}, u32[]{:S(2)}, u32[]{:S(2)}) collective-permute-start(f32[2,1,64,128]{3,2,1,0:T(8,128)} %stack.367), channel_id=1, source_target_pairs={{0,1},{1,2},{2,3},{3,4},{4,5},{5,6},{6,7},{7,8},{8,9},{9,10},{10,1... | collective-permute-start | bytes 196616 | tf_op jit(solution)/shard_map/ppermute | solution.py:18
  74.6 5.6 %collective-permute-start.2 = (f32[2,1,64,128]{3,2,1,0:T(8,128)S(1)}, f32[2,1,64,128]{3,2,1,0:T(8,128)S(1)}, u32[]{:S(2)}, u32[]{:S(2)}) collective-permute-start(f32[2,1,64,128]{3,2,1,0:T(8,128)S(1)} %pad_maximum_fusion.18), channel_id=1, source_target_pairs={{0,1},{1,2},{2,3},{3,4},{4,5},{5,6},{6,7},{7,8},{8,9},{9,10},{10,1... | collective-permute-start | bytes 196616 | tf_op jit(solution)/shard_map/ppermute | solution.py:18
  81.4 3.1 collective-permute-start.3
  84.7 6.3 %collective-permute-start.4 = (f32[2,1,64,128]{3,2,1,0:T(8,128)S(1)}, f32[2,1,64,128]{3,2,1,0:T(8,128)S(1)}, u32[]{:S(2)}, u32[]{:S(2)}) collective-permute-start(f32[2,1,64,128]{3,2,1,0:T(8,128)S(1)} %pad_maximum_fusion.20), channel_id=1, source_target_pairs={{0,1},{1,2},{2,3},{3,4},{4,5},{5,6},{6,7},{7,8},{8,9},{9,10},{10,1... | collective-permute-start | bytes 196616 | tf_op jit(solution)/shard_map/ppermute | solution.py:18
  92.2 3.1 collective-permute-start.5
  95.6 7.1 %collective-permute-start.6 = (f32[2,1,64,128]{3,2,1,0:T(8,128)S(1)}, f32[2,1,64,128]{3,2,1,0:T(8,128)S(1)}, u32[]{:S(2)}, u32[]{:S(2)}) collective-permute-start(f32[2,1,64,128]{3,2,1,0:T(8,128)S(1)} %pad_maximum_fusion.22), channel_id=1, source_target_pairs={{0,1},{1,2},{2,3},{3,4},{4,5},{5,6},{6,7},{7,8},{8,9},{9,10},{10,1... | collective-permute-start | bytes 196616 | tf_op jit(solution)/shard_map/ppermute | solution.py:18
  103.9 3.1 collective-permute-start.7
  107.2 7.2 %collective-permute-start.8 = (f32[2,1,64,128]{3,2,1,0:T(8,128)S(1)}, f32[2,1,64,128]{3,2,1,0:T(8,128)S(1)}, u32[]{:S(2)}, u32[]{:S(2)}) collective-permute-start(f32[2,1,64,128]{3,2,1,0:T(8,128)S(1)} %pad_maximum_fusion.24), channel_id=1, source_target_pairs={{0,1},{1,2},{2,3},{3,4},{4,5},{5,6},{6,7},{7,8},{8,9},{9,10},{10,1... | collective-permute-start | bytes 196616 | tf_op jit(solution)/shard_map/ppermute | solution.py:18
  115.6 3.1 collective-permute-start.9
  118.9 7.2 %collective-permute-start.10 = (f32[2,1,64,128]{3,2,1,0:T(8,128)S(1)}, f32[2,1,64,128]{3,2,1,0:T(8,128)S(1)}, u32[]{:S(2)}, u32[]{:S(2)}) collective-permute-start(f32[2,1,64,128]{3,2,1,0:T(8,128)S(1)} %pad_maximum_fusion.26), channel_id=1, source_target_pairs={{0,1},{1,2},{2,3},{3,4},{4,5},{5,6},{6,7},{7,8},{8,9},{9,10},{10,1... | collective-permute-start | bytes 196616 | tf_op jit(solution)/shard_map/ppermute | solution.py:18
  127.3 3.1 collective-permute-start.11
  130.6 7.2 %collective-permute-start.12 = (f32[2,1,64,128]{3,2,1,0:T(8,128)S(1)}, f32[2,1,64,128]{3,2,1,0:T(8,128)S(1)}, u32[]{:S(2)}, u32[]{:S(2)}) collective-permute-start(f32[2,1,64,128]{3,2,1,0:T(8,128)S(1)} %pad_maximum_fusion.28), channel_id=1, source_target_pairs={{0,1},{1,2},{2,3},{3,4},{4,5},{5,6},{6,7},{7,8},{8,9},{9,10},{10,1... | collective-permute-start | bytes 196616 | tf_op jit(solution)/shard_map/ppermute | solution.py:18
  139.1 3.1 collective-permute-start.13
  142.4 7.2 %collective-permute-start.14 = (f32[2,1,64,128]{3,2,1,0:T(8,128)S(1)}, f32[2,1,64,128]{3,2,1,0:T(8,128)S(1)}, u32[]{:S(2)}, u32[]{:S(2)}) collective-permute-start(f32[2,1,64,128]{3,2,1,0:T(8,128)S(1)} %pad_maximum_fusion.30), channel_id=1, source_target_pairs={{0,1},{1,2},{2,3},{3,4},{4,5},{5,6},{6,7},{7,8},{8,9},{9,10},{10,1... | collective-permute-start | bytes 196616 | tf_op jit(solution)/shard_map/ppermute | solution.py:18
  192.5 3.1 collective-permute-start.16
  195.9 4.7 %collective-permute-start.17 = (f32[2,1,64,128]{3,2,1,0:T(8,128)S(1)}, f32[2,1,64,128]{3,2,1,0:T(8,128)S(1)}, u32[]{:S(2)}, u32[]{:S(2)}) collective-permute-start(f32[2,1,64,128]{3,2,1,0:T(8,128)S(1)} %pad_maximum_fusion.32), channel_id=1, source_target_pairs={{0,1},{1,2},{2,3},{3,4},{4,5},{5,6},{6,7},{7,8},{8,9},{9,10},{10,1... | collective-permute-start | bytes 196616 | tf_op jit(solution)/shard_map/ppermute | solution.py:18
  201.7 3.1 collective-permute-start.18
  205.0 6.3 %collective-permute-start.19 = (f32[2,1,64,128]{3,2,1,0:T(8,128)S(1)}, f32[2,1,64,128]{3,2,1,0:T(8,128)S(1)}, u32[]{:S(2)}, u32[]{:S(2)}) collective-permute-start(f32[2,1,64,128]{3,2,1,0:T(8,128)S(1)} %pad_maximum_fusion.34), channel_id=1, source_target_pairs={{0,1},{1,2},{2,3},{3,4},{4,5},{5,6},{6,7},{7,8},{8,9},{9,10},{10,1... | collective-permute-start | bytes 196616 | tf_op jit(solution)/shard_map/ppermute | solution.py:18
  215.9 6.3 %collective-permute-start.21 = (f32[2,1,64,128]{3,2,1,0:T(8,128)S(1)}, f32[2,1,64,128]{3,2,1,0:T(8,128)S(1)}, u32[]{:S(2)}, u32[]{:S(2)}) collective-permute-start(f32[2,1,64,128]{3,2,1,0:T(8,128)S(1)} %pad_maximum_fusion.36), channel_id=1, source_target_pairs={{0,1},{1,2},{2,3},{3,4},{4,5},{5,6},{6,7},{7,8},{8,9},{9,10},{10,1... | collective-permute-start | bytes 196616 | tf_op jit(solution)/shard_map/ppermute | solution.py:18
  226.7 6.3 %collective-permute-start.23 = (f32[2,1,64,128]{3,2,1,0:T(8,128)S(1)}, f32[2,1,64,128]{3,2,1,0:T(8,128)S(1)}, u32[]{:S(2)}, u32[]{:S(2)}) collective-permute-start(f32[2,1,64,128]{3,2,1,0:T(8,128)S(1)} %pad_maximum_fusion.38), channel_id=1, source_target_pairs={{0,1},{1,2},{2,3},{3,4},{4,5},{5,6},{6,7},{7,8},{8,9},{9,10},{10,1... | collective-permute-start | bytes 196616 | tf_op jit(solution)/shard_map/ppermute | solution.py:18
  237.4 6.3 %collective-permute-start.25 = (f32[2,1,64,128]{3,2,1,0:T(8,128)S(1)}, f32[2,1,64,128]{3,2,1,0:T(8,128)S(1)}, u32[]{:S(2)}, u32[]{:S(2)}) collective-permute-start(f32[2,1,64,128]{3,2,1,0:T(8,128)S(1)} %pad_maximum_fusion.40), channel_id=1, source_target_pairs={{0,1},{1,2},{2,3},{3,4},{4,5},{5,6},{6,7},{7,8},{8,9},{9,10},{10,1... | collective-permute-start | bytes 196616 | tf_op jit(solution)/shard_map/ppermute | solution.py:18
  248.2 6.3 %collective-permute-start.27 = (f32[2,1,64,128]{3,2,1,0:T(8,128)S(1)}, f32[2,1,64,128]{3,2,1,0:T(8,128)S(1)}, u32[]{:S(2)}, u32[]{:S(2)}) collective-permute-start(f32[2,1,64,128]{3,2,1,0:T(8,128)S(1)} %pad_maximum_fusion.42), channel_id=1, source_target_pairs={{0,1},{1,2},{2,3},{3,4},{4,5},{5,6},{6,7},{7,8},{8,9},{9,10},{10,1... | collective-permute-start | bytes 196616 | tf_op jit(solution)/shard_map/ppermute | solution.py:18
  259.1 7.2 %collective-permute-start.29 = (f32[2,1,64,128]{3,2,1,0:T(8,128)S(1)}, f32[2,1,64,128]{3,2,1,0:T(8,128)S(1)}, u32[]{:S(2)}, u32[]{:S(2)}) collective-permute-start(f32[2,1,64,128]{3,2,1,0:T(8,128)S(1)} %pad_maximum_fusion.44), channel_id=1, source_target_pairs={{0,1},{1,2},{2,3},{3,4},{4,5},{5,6},{6,7},{7,8},{8,9},{9,10},{10,1... | collective-permute-start | bytes 196616 | tf_op jit(solution)/shard_map/ppermute | solution.py:18
  (68 other events, 441.1 us)
where the time goes:
time: 321 us; the launch traced here: 320 us
  starting transfers between devices  105 us (33%)
  blocking collectives  97.6 us (30%)
  other arithmetic  39.6 us (12%)
  local copies, waits for them, and re-layouts  36.9 us (11%)
  waiting for transfers between devices  36.3 us (11%)
  between operations  4.26 us (1%)
    ppermute x30, starting transfers between devices, from_behind(): return lax.ppermute(x, axis, pairs)  105 us
    ppermute x30, waiting for transfers between devices, from_behind(): return lax.ppermute(x, axis, pairs)  36.3 us
    psum x1, blocking collectives, local(): lax.psum((intersection_re, intersection_im, power), 'domain')  30.6 us
    psum x1, blocking collectives, local(): summed = lax.psum(partial_grads, 'domain')  30 us
    all_gather x1, blocking collectives, local(): lax.all_gather(permittivity, 'domain', axis=1, tiled=True)  19.5 us
    all_gather x1, blocking collectives, local(): lax.all_gather(conductivity, 'domain', axis=1, tiled=True)  17.5 us
    add x28, other arithmetic, new_electric(): updated.append(keep_rate[c] * electric[c] + gain_rate[c] * pushing)  14.3 us
    reshape x2, local copies, waits for them, and re-layouts, local(): cellwise.reshape(6, width, rows_y // 8, 8, rows_z // 8, 8).sum(axis=(3, 5))  8.87 us
  transfers between devices with their start and end apart: 30, of which 28 were waited for; matrix products, arithmetic and copies ran while one was open for 6% of the time, Pallas kernels for 0%

commit v1 on v0

v1 whole, which is shorter than its diff:
```python
import functools
import math

import jax
import jax.numpy as jnp
from jax import lax
from jax.experimental import pallas as pl
from jax.experimental.pallas import tpu as pltpu
from jax.sharding import PartitionSpec as P

STEPS = 8
NF = 4
MESH = pl.DeviceIdType.MESH
HIGH = lax.Precision.HIGHEST


def kernel(
    nd,
    planes_ref,
    coef_ref,
    e_hbm,
    h_hbm,
    ae_hbm,
    ah_hbm,
    tab_ref,
    lab_ref,
    packed_ref,
    src_ref,
    mon_ref,
    out_ref,
    hist,
    mag,
    send_r,
    send_l,
    recv_r,
    recv_l,
    rates,
    ghost,
    green,
    green_h,
    green_rates,
    tabs,
    labs,
    mids,
    ends,
    cells,
    tab_all,
    mid_own,
    end_own,
    load_sem,
    sr_sem,
    sl_sem,
    rr_sem,
    rl_sem,
    g_send,
    g_recv,
):
    width = lab_ref.shape[0]
    rows, lanes = src_ref.shape
    blocks = rows // 8
    regions = tab_ref.shape[1]
    per = regions // nd
    layers = nd * width
    me = lax.axis_index("domain")
    last = width - 1
    reach = STEPS - 1
    source = planes_ref[0]
    monitor = planes_ref[1]

    loads = []
    for r, (e, h) in enumerate(((e_hbm, h_hbm), (ae_hbm, ah_hbm))):
        loads.append(pltpu.make_async_copy(e, hist.at[r, 0], load_sem.at[2 * r]))
        loads.append(pltpu.make_async_copy(h, mag.at[r], load_sem.at[2 * r + 1]))
    for load in loads:
        load.start()

    barrier = pltpu.get_barrier_semaphore()

    def greet(j, carry):
        pl.semaphore_signal(
            barrier, inc=1, device_id={"domain": lax.rem(me + j, nd)}, device_id_type=MESH
        )
        return carry

    lax.fori_loop(1, nd, greet, 0)

    def to_all(phase, own, slots):
        def copy(j, away):
            return pltpu.make_async_remote_copy(
                src_ref=own,
                dst_ref=slots.at[away],
                send_sem=g_send.at[phase, j],
                recv_sem=g_recv.at[phase, j],
                device_id={"domain": lax.rem(me + j, nd)},
                device_id_type=MESH,
            )

        def begin():
            def one(j, carry):
                copy(j, me).start()
                return carry

            lax.fori_loop(1, nd, one, 0)

        def end():
            def one(j, carry):
                copy(j, me).wait_send()
                copy(j, lax.rem(me + nd - j, nd)).wait_recv()
                return carry

            lax.fori_loop(1, nd, one, 0)

        return begin, end

    tab_begin, tab_end = to_all(0, tab_ref, tabs)
    lab_begin, lab_end = to_all(1, lab_ref, labs)
    mid_begin, mid_end = to_all(2, mid_own, mids)
    end_begin, end_end = to_all(3, end_own, ends)

    pl.semaphore_wait(barrier, nd - 1)
    tab_begin()
    lab_begin()
    tabs[me] = tab_ref[...]
    labs[me] = lab_ref[...]

    row_at = lax.broadcasted_iota(jnp.int32, (rows, lanes), 0)
    lane_at = lax.broadcasted_iota(jnp.int32, (rows, lanes), 1)

    def lag_j(x):
        return jnp.where(row_at == 0, 0.0, pltpu.roll(x, 1, 0))

    def lag_k(x):
        return jnp.where(lane_at == 0, 0.0, pltpu.roll(x, 1, 1))

    def lead_j(x):
        return jnp.where(row_at == rows - 1, 0.0, pltpu.roll(x, rows - 1, 0))

    def lead_k(x):
        return jnp.where(lane_at == lanes - 1, 0.0, pltpu.roll(x, lanes - 1, 1))

    @pl.when(me == 0)
    def _():
        recv_r[...] = jnp.zeros_like(recv_r)

    @pl.when(me == nd - 1)
    def _():
        recv_l[...] = jnp.zeros_like(recv_l)

    def clear(w, carry):
        zero = jnp.zeros((rows, lanes), jnp.float32)
        for k in range(STEPS):
            for c in range(3):
                green[k, c, w] = zero
        for c in range(3):
            green_h[c, w] = zero
        return carry

    lax.fori_loop(0, 2 * reach + 3, clear, 0)

    tab_end()
    lab_end()

    def add_tab(s, acc):
        return acc + tabs[s]

    tab_all[...] = lax.fori_loop(1, nd, add_tab, tabs[0])

    def looked_up(c, label):
        value = jnp.zeros(label.shape, jnp.float32)
        for q in range(regions // lanes):
            row = jnp.broadcast_to(tab_all[c : c + 1, q * lanes : (q + 1) * lanes], label.shape)
            found = jnp.take_along_axis(row, lax.rem(label, lanes), axis=1)
            value = jnp.where(lax.div(label, lanes) == q, found, value)
        return value

    def rates_of(c, label):
        perm = looked_up(c, label)
        cond = looked_up(3 + c, label)
        loss = cond * 0.5 / perm
        return (1.0 - loss) / (1.0 + loss), 1.0 / (perm * (1.0 + loss))

    def spread(write, value):
        for b in range(blocks):
            write(b, jnp.broadcast_to(value[b : b + 1], (8, lanes)))

    for l in range(width):
        for c in range(3):
            keep, gain = rates_of(c, lab_ref[l])

            def put(b, v, c=c, l=l):
                rates[c, l, pl.ds(b * 8, 8)] = v

            def put_gain(b, v, c=c, l=l):
                rates[3 + c, l, pl.ds(b * 8, 8)] = v

            spread(put, keep)
            spread(put_gain, gain)

    after = lax.rem(me + 1, nd)
    inside = jnp.where(me == nd - 1, 0.0, 0.5)
    for c in (1, 2):
        _, gain = rates_of(c, labs[after, 0])

        def put_ghost(b, v, c=c):
            ghost[c - 1, pl.ds(b * 8, 8)] = v * inside

        spread(put_ghost, gain)

    for load in loads:
        load.wait()

    def forcing_at(n, l):
        lit = jnp.where(source == me * width + l, coef_ref[2, n], 0.0)
        return src_ref[...] * lit

    def make_edge(r, n):
        for c in (1, 2):
            send_r[r, n, c - 1] = mag[r, c, last]
        hx, hy, hz = mag[r, 0, 0], mag[r, 1, 0], mag[r, 2, 0]
        py = rates[1, 0] * hist[r, n, 1, 0] + rates[4, 0] * (0.5 * (hx - lag_k(hx) - hz))
        push = 0.5 * (hy - (hx - lag_j(hx)))
        if r == 0:
            push = push - forcing_at(n, 0)
        pz = rates[2, 0] * hist[r, n, 2, 0] + rates[5, 0] * push
        send_l[r, n, 0] = py
        send_l[r, n, 1] = pz

    def right_copy(r, n):
        return pltpu.make_async_remote_copy(
            src_ref=send_r.at[r, n],
            dst_ref=recv_r.at[r, n],
            send_sem=sr_sem.at[r, n],
            recv_sem=rr_sem.at[r, n],
            device_id={"domain": lax.rem(me + 1, nd)},
            device_id_type=MESH,
        )

    def left_copy(r, n):
        return pltpu.make_async_remote_copy(
            src_ref=send_l.at[r, n],
            dst_ref=recv_l.at[r, n],
            send_sem=sl_sem.at[r, n],
            recv_sem=rl_sem.at[r, n],
            device_id={"domain": lax.rem(me + nd - 1, nd)},
            device_id_type=MESH,
        )

    def start_edge(r, n):
        @pl.when(me < nd - 1)
        def _():
            right_copy(r, n).start()

        @pl.when((me > 0) & (n < STEPS - 1))
        def _():
            left_copy(r, n).start()

    def wait_right(r, n):
        @pl.when(me > 0)
        def _():
            right_copy(r, n).wait_recv()

    def wait_left(r, n):
        @pl.when(me < nd - 1)
        def _():
            left_copy(r, n).wait_recv()

    def electric_inner(r, n):
        for l in range(width):
            hx, hy, hz = mag[r, 0, l], mag[r, 1, l], mag[r, 2, l]
            hist[r, n + 1, 0, l] = rates[0, l] * hist[r, n, 0, l] + rates[3, l] * (
                0.5 * (hz - lag_j(hz) - (hy - lag_k(hy)))
            )
            if l == 0:
                continue
            hist[r, n + 1, 1, l] = rates[1, l] * hist[r, n, 1, l] + rates[4, l] * (
                0.5 * (hx - lag_k(hx) - (hz - mag[r, 2, l - 1]))
            )
            push = 0.5 * (hy - mag[r, 1, l - 1] - (hx - lag_j(hx)))
            if r == 0:
                push = push - forcing_at(n, l)
            hist[r, n + 1, 2, l] = rates[2, l] * hist[r, n, 2, l] + rates[5, l] * push

    def electric_first(r, n):
        hist[r, n + 1, 1, 0] = send_l[r, n, 0] + rates[4, 0] * (0.5 * recv_r[r, n, 1])
        hist[r, n + 1, 2, 0] = send_l[r, n, 1] - rates[5, 0] * (0.5 * recv_r[r, n, 0])

    def magnetic_at(r, n, l, ey_right, ez_right):
        ex, ey, ez = hist[r, n + 1, 0, l], hist[r, n + 1, 1, l], hist[r, n + 1, 2, l]
        mag[r, 0, l] = mag[r, 0, l] - 0.5 * (lead_j(ez) - ez - (lead_k(ey) - ey))
        mag[r, 1, l] = mag[r, 1, l] - 0.5 * (lead_k(ex) - ex - (ez_right - ez))
        mag[r, 2, l] = mag[r, 2, l] - 0.5 * (ey_right - ey - (lead_j(ex) - ex))

    def magnetic_last(r, n):
        ey = recv_l[r, n, 0] + ghost[0] * mag[r, 2, last]
        ez = recv_l[r, n, 1] - ghost[1] * mag[r, 1, last]
        magnetic_at(r, n, last, ey, ez)

    def magnetic_inner(r, n, l):
        magnetic_at(r, n, l, hist[r, n + 1, 1, l + 1], hist[r, n + 1, 2, l + 1])

    for r in range(2):
        make_edge(r, 0)
        start_edge(r, 0)

    def green_layer(w, carry):
        at = monitor - reach + w
        ok = (at >= 0) & (at < layers)
        place = jnp.clip(at, 0, layers - 1)
        label = labs[lax.div(place, width), lax.rem(place, width)]
        for c in range(3):
            keep, gain = rates_of(c, label)
            keep = jnp.where(ok, keep, 0.0)
            gain = jnp.where(ok, gain, 0.0)

            def put(b, v, c=c):
                green_rates[c, w, pl.ds(b * 8, 8)] = v

            def put_gain(b, v, c=c):
                green_rates[3 + c, w, pl.ds(b * 8, 8)] = v

            spread(put, keep)
            spread(put_gain, gain)
        return carry

    lax.fori_loop(0, 2 * reach + 1, green_layer, 0)
    green[0, 1, reach + 1] = -(green_rates[4, reach] * mon_ref[...])

    def green_magnetic(k):
        def one(w, carry):
            at = monitor - reach + w - 1
            half = jnp.where((at >= 0) & (at < layers), 0.5, 0.0)
            ex, ey, ez = green[k, 0, w], green[k, 1, w], green[k, 2, w]
            green_h[0, w] = green_h[0, w] - half * (lead_j(ez) - ez - (lead_k(ey) - ey))
            green_h[1, w] = green_h[1, w] - half * (lead_k(ex) - ex - (green[k, 2, w + 1] - ez))
            green_h[2, w] = green_h[2, w] - half * (green[k, 1, w + 1] - ey - (lead_j(ex) - ex))
            return carry

        lax.fori_loop(reach - k, reach + 2 + k, one, 0)

    def green_electric(k):
        def one(w, carry):
            hx, hy, hz = green_h[0, w], green_h[1, w], green_h[2, w]
            green[k, 0, w] = green_rates[0, w - 1] * green[k - 1, 0, w] + green_rates[3, w - 1] * (
                0.5 * (hz - lag_j(hz) - (hy - lag_k(hy)))
            )
            green[k, 1, w] = green_rates[1, w - 1] * green[k - 1, 1, w] + green_rates[4, w - 1] * (
                0.5 * (hx - lag_k(hx) - (hz - green_h[2, w - 1]))
            )
            green[k, 2, w] = green_rates[2, w - 1] * green[k - 1, 2, w] + green_rates[5, w - 1] * (
                0.5 * (hy - green_h[1, w - 1] - (hx - lag_j(hx)))
            )
            return carry

        lax.fori_loop(reach + 1 - k, reach + 2 + k, one, 0)

    def step(n, carry):
        for r in range(2):
            electric_inner(r, n)
        green_magnetic(n)
        green_electric(n + 1)
        for r in range(2):
            wait_right(r, n)
            electric_first(r, n)
            wait_left(r, n)
            magnetic_last(r, n)
            magnetic_inner(r, n, 0)
            make_edge(r, n + 1)
            start_edge(r, n + 1)
        for r in range(2):
            for l in range(1, last):
                magnetic_inner(r, n, l)
        return carry

    lax.fori_loop(0, STEPS - 1, step, 0)
    n = STEPS - 1
    for r in range(2):
        electric_inner(r, n)
    for r in range(2):
        wait_right(r, n)
        electric_first(r, n)

    mon_at = monitor - me * width
    mon_ok = jnp.where((mon_at >= 0) & (mon_at < width), 1.0, 0.0)
    mon_at = jnp.clip(mon_at, 0, width - 1)
    src_at = source - me * width
    src_ok = jnp.where((src_at >= 0) & (src_at < width), 1.0 / (rows * lanes), 0.0)
    src_at = jnp.clip(src_at, 0, width - 1)
    for t in range(STEPS):
        prod = hist[0, t + 1, 1, mon_at] * mon_ref[...]
        mid_own[t : t + 1] = jnp.sum(prod, axis=0, keepdims=True) * mon_ok
    for f in range(NF):
        re = jnp.zeros((rows, lanes), jnp.float32)
        im = jnp.zeros((rows, lanes), jnp.float32)
        for t in range(STEPS):
            field = hist[0, t + 1, 2, src_at]
            re = re + coef_ref[4 + f, t] * field
            im = im - coef_ref[8 + f, t] * field
        mid_own[STEPS + f : STEPS + f + 1] = (
            jnp.sum(re * re + im * im, axis=0, keepdims=True) * src_ok
        )
    mid_own[STEPS + NF :] = jnp.zeros((16 - STEPS - NF, lanes), jnp.float32)
    mid_begin()
    mids[me] = mid_own[...]
    mid_end()

    def add_mid(s, acc):
        return acc + mids[s]

    total = lax.fori_loop(1, nd, add_mid, mids[0])
    total = jnp.broadcast_to(jnp.sum(total, axis=1, keepdims=True), (16, lanes))
    root = 1.0 / math.sqrt(rows * lanes)
    amp = []
    for f in range(NF):
        scale = root / jnp.sqrt(total[STEPS + f : STEPS + f + 1] + 1e-06)
        re = jnp.zeros((1, lanes), jnp.float32)
        im = jnp.zeros((1, lanes), jnp.float32)
        for t in range(STEPS):
            re = re + coef_ref[4 + f, t] * total[t : t + 1]
            im = im - coef_ref[8 + f, t] * total[t : t + 1]
        amp.append((re * scale, im * scale))
    drive = []
    for t in range(STEPS):
        s = jnp.zeros((1, lanes), jnp.float32)
        for f in range(NF):
            s = s + amp[f][0] * coef_ref[4 + f, t] + amp[f][1] * coef_ref[8 + f, t]
        drive.append(jnp.broadcast_to(s, (8, lanes)))

    for l in range(width):
        w = me * width + l - monitor + reach + 1
        w = jnp.where((w >= 1) & (w <= 2 * reach + 1), w, 0)

        def correlate(i, carry, l=l, w=w):
            c = lax.div(i, blocks)
            b = lax.rem(i, blocks)
            at = pl.ds(pl.multiple_of(b * 8, 8), 8)
            first = [hist[0, t + 1, c, l, at] for t in range(STEPS)]
            impulse = [green[t, c, w, at] for t in range(STEPS)]
            second = []
            for t in range(STEPS):
                a = hist[1, t + 1, c, l, at]
                for m in range(t + 1):
                    a = a + drive[m] * impulse[t - m]
                second.append(a)
            perm = jnp.zeros((8, lanes), jnp.float32)
            cond = jnp.zeros((8, lanes), jnp.float32)
            for p in range(2 * STEPS - 1):
                q = None
                for t in range(max(0, p - STEPS + 1), min(p, STEPS - 1) + 1):
                    term = first[t] * second[p - t]
                    q = term if q is None else q + term
                perm = perm + coef_ref[0, p] * q
                cond = cond + coef_ref[1, p] * q
            cells[c, l, pl.ds(b, 1)] = jnp.sum(perm, axis=0, keepdims=True)
            cells[3 + c, l, pl.ds(b, 1)] = jnp.sum(cond, axis=0, keepdims=True)
            return carry

        lax.fori_loop(0, 3 * blocks, correlate, 0)

    left = lax.broadcasted_iota(jnp.int32, (lanes, lanes), 0)
    up = lax.broadcasted_iota(jnp.int32, (lanes, lanes), 1)
    pool = (lax.div(left, 8) == lax.div(up, 8)).astype(jnp.float32)
    flat = cells[...].reshape(6 * width * blocks, lanes)
    pooled = jnp.dot(flat, pool, precision=HIGH, preferred_element_type=jnp.float32)
    pooled = pooled.reshape(6 * width, blocks, lanes)
    sub = lax.broadcasted_iota(jnp.int32, (blocks, lanes), 0)
    lane = lax.broadcasted_iota(jnp.int32, (blocks, lanes), 1)
    mine = lax.rem(lane, 8) == sub
    packed = jnp.sum(jnp.where(mine[None], pooled, 0.0), axis=1).reshape(6, width, lanes)
    region = lax.broadcasted_iota(jnp.int32, (regions, lanes), 0)
    partial = jnp.zeros((8, regions), jnp.float32)
    for l in range(width):
        hot = (region == jnp.broadcast_to(packed_ref[l : l + 1], (regions, lanes))).astype(
            jnp.float32
        )
        these = jnp.concatenate([packed[:, l], jnp.zeros((2, lanes), jnp.float32)], axis=0)
        partial = partial + lax.dot_general(
            these, hot, (((1,), (1,)), ((), ())), precision=HIGH, preferred_element_type=jnp.float32
        )
    end_own[...] = partial * math.sqrt(regions / (layers * rows * lanes))
    end_begin()
    ends[me] = end_own[...]
    end_end()

    def add_end(s, acc):
        return acc + ends[s]

    summed = lax.fori_loop(1, nd, add_end, ends[0])
    chosen = lax.broadcasted_iota(jnp.int32, (regions, lanes), 0)
    wanted = lax.broadcasted_iota(jnp.int32, (regions, lanes), 1) + me * per
    pick = ((chosen == wanted) & (wanted < (me + 1) * per)).astype(jnp.float32)
    out_ref[...] = jnp.dot(summed, pick, precision=HIGH, preferred_element_type=jnp.float32)

    for r in range(2):

        def done(n, carry, r=r):
            @pl.when(me < nd - 1)
            def _():
                right_copy(r, n).wait_send()

            @pl.when((me > 0) & (n < STEPS - 1))
            def _():
                left_copy(r, n).wait_send()

            return carry

        lax.fori_loop(0, STEPS, done, 0)


def local(nd, e, h, ae, ah, perm, cond, labels, source, monitor, wave, src_mode, mon_mode):
    width, blocks = labels.shape[0], labels.shape[1]
    rows, lanes = src_mode.shape
    per = perm.shape[1]
    regions = nd * per
    me = lax.axis_index("domain")
    both = jnp.concatenate([perm, cond, jnp.zeros((2, per), jnp.float32)], 0)
    own = lax.div(jnp.arange(regions, dtype=jnp.int32), per) == me
    tab = jnp.where(own[None], jnp.tile(both, (1, nd)), 0.0)
    lab = jnp.repeat(labels, 8, axis=2)
    packed = jnp.transpose(labels, (0, 2, 1)).reshape(width, lanes)
    packed = jnp.concatenate([packed, jnp.zeros((-width % 8, lanes), jnp.int32)], 0)
    omega = 0.25 + 0.05 * wave.astype(jnp.float32)
    sums = jnp.arange(2, 2 * STEPS + 2).astype(jnp.float32)
    angle = omega[:, None] * sums[None]
    times = omega[:, None] * (jnp.arange(16).astype(jnp.float32) + 1.0)[None]
    coef = jnp.concatenate(
        [
            jnp.sum((omega * omega)[:, None] * jnp.cos(angle), axis=0)[None],
            -jnp.sum(omega[:, None] * jnp.sin(angle), axis=0)[None],
            jnp.sum(jnp.sin(times), axis=0)[None],
            jnp.zeros((1, 16), jnp.float32),
            jnp.cos(times),
            jnp.sin(times),
        ],
        0,
    )
    planes = jnp.concatenate([source, monitor])
    f32 = jnp.float32
    span = 2 * (STEPS - 1) + 1
    smem = pl.BlockSpec(memory_space=pltpu.SMEM)
    vmem = pl.BlockSpec(memory_space=pltpu.VMEM)
    hbm = pl.BlockSpec(memory_space=pl.ANY)
    dma = pltpu.SemaphoreType.DMA
    edge = pltpu.VMEM((2, STEPS, 2, rows, lanes), f32)
    out = pl.pallas_call(
        functools.partial(kernel, nd),
        out_shape=jax.ShapeDtypeStruct((8, lanes), f32),
        in_specs=[smem, smem, hbm, hbm, hbm, hbm, vmem, vmem, vmem, vmem, vmem],
        out_specs=vmem,
        scratch_shapes=[
            pltpu.VMEM((2, STEPS + 1, 3, width, rows, lanes), f32),
            pltpu.VMEM((2, 3, width, rows, lanes), f32),
            edge,
            edge,
            edge,
            edge,
            pltpu.VMEM((6, width, rows, lanes), f32),
            pltpu.VMEM((2, rows, lanes), f32),
            pltpu.VMEM((STEPS, 3, span + 2, rows, lanes), f32),
            pltpu.VMEM((3, span + 2, rows, lanes), f32),
            pltpu.VMEM((6, span, rows, lanes), f32),
            pltpu.VMEM((nd, 8, regions), f32),
            pltpu.VMEM((nd, width, blocks, lanes), jnp.int32),
            pltpu.VMEM((nd, 16, lanes), f32),
            pltpu.VMEM((nd, 8, regions), f32),
            pltpu.VMEM((6, width, blocks, lanes), f32),
            pltpu.VMEM((8, regions), f32),
            pltpu.VMEM((16, lanes), f32),
            pltpu.VMEM((8, regions), f32),
            dma((4,)),
            dma((2, STEPS)),
            dma((2, STEPS)),
            dma((2, STEPS)),
            dma((2, STEPS)),
            dma((4, nd)),
            dma((4, nd)),
        ],
        compiler_params=pltpu.CompilerParams(
            collective_id=0, has_side_effects=True, vmem_limit_bytes=60 * 1024 * 1024
        ),
    )(planes, coef, e, h, ae, ah, tab, lab, packed, src_mode, mon_mode)
    return out[:6, :per]


def solution(mesh):
    placed = (
        P(None, ("design", "domain"), None, None),
        P(None, ("design", "domain"), None, None),
        P(None, ("design", "domain"), None, None),
        P(None, ("design", "domain"), None, None),
        P(None, ("design", "domain")),
        P(None, ("design", "domain")),
        P(("design", "domain"), None, None),
        P("design"),
        P("design"),
        P("design"),
        P("design", None),
        P("design", None),
    )
    return jax.shard_map(
        functools.partial(local, mesh.shape["domain"]),
        mesh=mesh,
        in_specs=placed,
        out_specs=P(None, ("design", "domain")),
        check_vma=False,
    )
```

time: 321 us -> 70.5 us (0.22)
  starting transfers between devices: 105 us -> 0 us
  blocking collectives: 97.6 us -> 0 us
  Pallas kernels: 0 us -> 61.9 us
  other arithmetic: 39.6 us -> 2.09 us
  waiting for transfers between devices: 36.3 us -> 0 us
  local copies, waits for them, and re-layouts: 36.9 us -> 4.89 us
    ppermute x30 -> x0, starting transfers between devices: 105 us -> none  [from_behind(): return lax.ppermute(x, axis, pairs)]
    pallas_call x0 -> x1, Pallas kernels: none -> 61.9 us  [local(): pl.pallas_call(functools.partial(kernel, nd), out_shape=jax.ShapeDtypeStr...]
    psum x2 -> x0, blocking collectives: 60.6 us -> none  [the longest x1 30.6 us: local(): lax.psum((intersection_re, intersection_im, power), 'domain')]
    all_gather x2 -> x0, blocking collectives: 37 us -> none  [the longest x1 19.5 us: local(): lax.all_gather(permittivity, 'domain', axis=1, tiled=True)]
    ppermute x30 -> x0, waiting for transfers between devices: 36.3 us -> none  [from_behind(): return lax.ppermute(x, axis, pairs)]
    add x29 -> x1, other arithmetic: 15.5 us -> 0.01 us  [local(): times = omega[:, None] * (jnp.arange(16).astype(jnp.float32) + 1.0)[None]]
    reduce_sum x6 -> x1, other arithmetic: 14.3 us -> 0.13 us  [local(): jnp.sum(omega[:, None] * jnp.sin(angle), axis=0)[None]]
    squeeze x90 -> x0, local copies, waits for them, and re-layouts: 9.35 us -> none  [the longest x32 5.8 us: evolve(): hz_left = jnp.concatenate([incoming[1], magnetic[2, :-1]], 0)]
  transfers between devices with their start and end apart: 30 -> 0, of which waited for: 28 -> 0; matrix products, arithmetic and copies ran while one was open for 6% -> 0% of each run, Pallas kernels for 0% -> 0%
where the time goes in v1:
time: 70.5 us; the launch traced here: 70.3 us
  Pallas kernels  61.9 us (88%)
  local copies, waits for them, and re-layouts  4.89 us (7%)
  other arithmetic  2.09 us (3%)
  between operations  1.37 us (2%)
    pallas_call x1, Pallas kernels, local(): pl.pallas_call(functools.partial(kernel, nd), out_shape=jax.ShapeDtypeStr...  61.9 us
    unnamed x7, local copies, waits for them, and re-layouts  1.88 us

profile of v1, /device:TPU:0, one launch (start us, length us, event | category | flops | bytes accessed | tf_op | source)
XLA Modules:
  0.0 70.3 jit_solution(14374336049396929389)
XLA Ops:
  0.0 0.7 fusion.5
  0.7 0.1 fusion.3
  0.8 0.0 copy-start
  0.8 1.2 %concatenate.13.coef_ref = f32[12,16]{1,0:T(8,128)} concatenate(f32[1,16]{1,0:T(1,128)S(1)} %bitcast.10, f32[1,16]{1,0:T(1,128)S(1)} %negate_bitcast_fusion, f32[1,16]{1,0:T(1,128)S(1)} %bitcast.11, f32[1,16]{1,0:T(1,128)S(1)} %broadcast.49, f32[4,16]{1,0:T(4,128)S(1)} %get-tuple-element.9, f32[4,16]{1,0:T(4,128)S(1)} %get-tuple-element.8), dimensions={0} | concatenate | bytes 1536 | tf_op jit(solution)/shard_map/concatenate | solution.py:525
  2.0 0.0 copy-done
  2.0 0.1 broadcast_in_dim.34
  2.2 0.0 copy-start.2
  2.2 0.7 %reshape.36.lab_ref = s32[4,8,128]{2,1,0:T(8,128)} reshape(s32[4,8,16,8]{3,2,1,0:T(8,128)S(1)} %broadcast_in_dim.34) | data formatting | bytes 32768 | tf_op jit(solution)/shard_map/reshape | solution.py:518
  2.9 0.0 copy-start.1
  2.9 0.1 pad.3.clone
  3.0 0.0 copy-done.2
  3.0 0.6 copy-done.1
  3.6 0.1 maximum_maximum_fusion
  3.7 0.1 tile.10
  3.8 0.6 broadcast_select_fusion.tab_ref
  4.4 0.1 copy.14
  4.5 0.1 reshape.37
  4.6 0.6 concatenate.15.packed_ref
  6.4 0.6 pad_add_fusion.planes_ref
  7.1 61.9 %shard_map.118 = f32[8,128]{1,0:T(8,128)} custom-call(s32[2]{0:T(128)} %pad_add_fusion.planes_ref, f32[12,16]{1,0:T(8,128)} %concatenate.13.coef_ref, f32[3,4,64,128]{3,2,1,0:T(8,128)} %e_hbm.1, f32[3,4,64,128]{3,2,1,0:T(8,128)} %h_hbm.1, f32[3,4,64,128]{3,2,1,0:T(8,128)} %ae_hbm.1, f32[3,4,64,128]{3,2,1,0:T(8,128)} %ah_hbm.1, ...), custom_call_target="tpu_custom_call" | custom-call | tf_op jit(solution)/shard_map/pallas_call | solution.py:544
  69.0 1.3 %copy.18 = f32[6,8]{1,0:T(8,128)} copy(f32[6,8]{1,0:T(8,128)} %bitcast.9) | data formatting | bytes 384
  (7 shorter events, 0.0 us)
Async XLA Ops:
  0.8 1.2 %copy-start = (s32[4,8,16]{2,1,0:T(8,128)S(1)}, s32[4,8,16]{2,1,0:T(8,128)}, u32[]{:S(2)}) copy-start(s32[4,8,16]{2,1,0:T(8,128)} %param.18) | copy-start | bytes 6148
  2.2 0.8 %copy-start.2 = (f32[3,8]{1,0:T(4,128)S(1)}, f32[3,8]{1,0:T(4,128)}, u32[]{:S(2)}) copy-start(f32[3,8]{1,0:T(4,128)} %param.16) | copy-start | bytes 292
  2.9 0.7 copy-start.1

commit v2 on v1

--- a/solution.py
+++ b/solution.py
@@ -16,15 +16,16 @@
 
 def kernel(
     nd,
-    planes_ref,
-    coef_ref,
+    source_ref,
+    monitor_ref,
+    wave_ref,
     e_hbm,
     h_hbm,
     ae_hbm,
     ah_hbm,
-    tab_ref,
+    perm_ref,
+    cond_ref,
     lab_ref,
-    packed_ref,
     src_ref,
     mon_ref,
     out_ref,
@@ -39,12 +40,16 @@
     green,
     green_h,
     green_rates,
-    tabs,
-    labs,
+    facts,
     mids,
     ends,
     cells,
     tab_all,
+    fact_own,
+    wide,
+    cos_t,
+    sin_t,
+    corr,
     mid_own,
     end_own,
     load_sem,
@@ -58,14 +63,14 @@
     width = lab_ref.shape[0]
     rows, lanes = src_ref.shape
     blocks = rows // 8
-    regions = tab_ref.shape[1]
-    per = regions // nd
+    per = perm_ref.shape[1]
+    regions = nd * per
     layers = nd * width
     me = lax.axis_index("domain")
     last = width - 1
     reach = STEPS - 1
-    source = planes_ref[0]
-    monitor = planes_ref[1]
+    source = source_ref[0]
+    monitor = monitor_ref[0]
 
     loads = []
     for r, (e, h) in enumerate(((e_hbm, h_hbm), (ae_hbm, ah_hbm))):
@@ -112,16 +117,52 @@
 
         return begin, end
 
-    tab_begin, tab_end = to_all(0, tab_ref, tabs)
-    lab_begin, lab_end = to_all(1, lab_ref, labs)
-    mid_begin, mid_end = to_all(2, mid_own, mids)
-    end_begin, end_end = to_all(3, end_own, ends)
+    fact_begin, fact_end = to_all(0, fact_own, facts)
+    mid_begin, mid_end = to_all(1, mid_own, mids)
+    end_begin, end_end = to_all(2, end_own, ends)
+
+    tile_row = lax.broadcasted_iota(jnp.int32, (8, lanes), 0)
+    tile_lane = lax.broadcasted_iota(jnp.int32, (8, lanes), 1)
+    group = lax.div(tile_lane, 8)
+    in_group = lax.rem(tile_lane, 8)
+    by_lane = in_group == tile_row
+
+    def flattened(x, mask):
+        return jnp.sum(jnp.where(mask, x, 0.0), axis=0, keepdims=True)
+
+    wide[...] = jnp.zeros_like(wide)
+    wide[0, 0:3, 0:per] = perm_ref[...]
+    wide[0, 3:6, 0:per] = cond_ref[...]
+    for l in range(width):
+        wide[1 + l, 0:blocks, 0 : lab_ref.shape[2]] = lab_ref[l].astype(jnp.float32)
+    fact_own[...] = jnp.zeros_like(fact_own)
+    repeated = jnp.take_along_axis(wide[0], lax.rem(tile_lane, per), axis=1)
+    fact_own[0:1] = flattened(repeated, lax.div(tile_lane, per) == tile_row)
+    for l in range(width):
+        fact_own[1 + l : 2 + l] = flattened(
+            jnp.take_along_axis(wide[1 + l], group, axis=1), by_lane
+        )
 
     pl.semaphore_wait(barrier, nd - 1)
-    tab_begin()
-    lab_begin()
-    tabs[me] = tab_ref[...]
-    labs[me] = lab_ref[...]
+    fact_begin()
+    facts[me] = fact_own[...]
+
+    moment = (lax.broadcasted_iota(jnp.int32, (16, lanes), 0) + 1).astype(jnp.float32)
+    weigh_perm = jnp.zeros((16, lanes), jnp.float32)
+    weigh_cond = jnp.zeros((16, lanes), jnp.float32)
+    drive_fwd = jnp.zeros((16, lanes), jnp.float32)
+    for f in range(NF):
+        omega = 0.25 + 0.05 * wave_ref[f].astype(jnp.float32)
+        cosine = jnp.cos(moment * omega)
+        sine = jnp.sin(moment * omega)
+        cos_t[f] = cosine
+        sin_t[f] = sine
+        weigh_perm = weigh_perm + (omega * omega) * cosine
+        weigh_cond = weigh_cond - omega * sine
+        drive_fwd = drive_fwd + sine
+    corr[0] = weigh_perm
+    corr[1] = weigh_cond
+    corr[2] = drive_fwd
 
     row_at = lax.broadcasted_iota(jnp.int32, (rows, lanes), 0)
     lane_at = lax.broadcasted_iota(jnp.int32, (rows, lanes), 1)
@@ -157,13 +198,22 @@
 
     lax.fori_loop(0, 2 * reach + 3, clear, 0)
 
-    tab_end()
-    lab_end()
-
-    def add_tab(s, acc):
-        return acc + tabs[s]
-
-    tab_all[...] = lax.fori_loop(1, nd, add_tab, tabs[0])
+    fact_end()
+
+    each = lanes // per
+    seat = lax.broadcasted_iota(jnp.int32, (each, lanes), 0)
+    lane_of = lax.broadcasted_iota(jnp.int32, (each, lanes), 1)
+    for q in range(regions // lanes):
+        row = facts[q * each : (q + 1) * each, 0]
+        for c in range(6):
+            found = jnp.take_along_axis(row, c * per + lax.rem(lane_of, per), axis=1)
+            tab_all[c : c + 1, q * lanes : (q + 1) * lanes] = flattened(
+                found, lax.div(lane_of, per) == seat
+            )
+
+    def layer_labels(device, l):
+        row = jnp.broadcast_to(facts[device, pl.ds(1 + l, 1)], (blocks, lanes))
+        return jnp.take_along_axis(row, group * 8 + tile_row, axis=1).astype(jnp.int32)
 
     def looked_up(c, label):
         value = jnp.zeros(label.shape, jnp.float32)
@@ -184,8 +234,9 @@
             write(b, jnp.broadcast_to(value[b : b + 1], (8, lanes)))
 
     for l in range(width):
+        label = layer_labels(me, l)
         for c in range(3):
-            keep, gain = rates_of(c, lab_ref[l])
+            keep, gain = rates_of(c, label)
 
             def put(b, v, c=c, l=l):
                 rates[c, l, pl.ds(b * 8, 8)] = v
@@ -198,8 +249,9 @@
 
     after = lax.rem(me + 1, nd)
     inside = jnp.where(me == nd - 1, 0.0, 0.5)
+    label = layer_labels(after, 0)
     for c in (1, 2):
-        _, gain = rates_of(c, labs[after, 0])
+        _, gain = rates_of(c, label)
 
         def put_ghost(b, v, c=c):
             ghost[c - 1, pl.ds(b * 8, 8)] = v * inside
@@ -210,8 +262,8 @@
         load.wait()
 
     def forcing_at(n, l):
-        lit = jnp.where(source == me * width + l, coef_ref[2, n], 0.0)
-        return src_ref[...] * lit
+        lit = jnp.where(source == me * width + l, 1.0, 0.0)
+        return src_ref[...] * (corr[2, pl.ds(n, 1)] * lit)
 
     def make_edge(r, n):
         for c in (1, 2):
@@ -306,7 +358,7 @@
         at = monitor - reach + w
         ok = (at >= 0) & (at < layers)
         place = jnp.clip(at, 0, layers - 1)
-        label = labs[lax.div(place, width), lax.rem(place, width)]
+        label = layer_labels(lax.div(place, width), lax.rem(place, width))
         for c in range(3):
             keep, gain = rates_of(c, label)
             keep = jnp.where(ok, keep, 0.0)
@@ -373,11 +425,9 @@
 
     lax.fori_loop(0, STEPS - 1, step, 0)
     n = STEPS - 1
-    for r in range(2):
-        electric_inner(r, n)
-    for r in range(2):
-        wait_right(r, n)
-        electric_first(r, n)
+    electric_inner(0, n)
+    wait_right(0, n)
+    electric_first(0, n)
 
     mon_at = monitor - me * width
     mon_ok = jnp.where((mon_at >= 0) & (mon_at < width), 1.0, 0.0)
@@ -393,14 +443,17 @@
         im = jnp.zeros((rows, lanes), jnp.float32)
         for t in range(STEPS):
             field = hist[0, t + 1, 2, src_at]
-            re = re + coef_ref[4 + f, t] * field
-            im = im - coef_ref[8 + f, t] * field
+            re = re + cos_t[f, t : t + 1] * field
+            im = im - sin_t[f, t : t + 1] * field
         mid_own[STEPS + f : STEPS + f + 1] = (
             jnp.sum(re * re + im * im, axis=0, keepdims=True) * src_ok
         )
     mid_own[STEPS + NF :] = jnp.zeros((16 - STEPS - NF, lanes), jnp.float32)
     mid_begin()
     mids[me] = mid_own[...]
+    electric_inner(1, n)
+    wait_right(1, n)
+    electric_first(1, n)
     mid_end()
 
     def add_mid(s, acc):
@@ -415,14 +468,14 @@
         re = jnp.zeros((1, lanes), jnp.float32)
         im = jnp.zeros((1, lanes), jnp.float32)
         for t in range(STEPS):
-            re = re + coef_ref[4 + f, t] * total[t : t + 1]
-            im = im - coef_ref[8 + f, t] * total[t : t + 1]
+            re = re + cos_t[f, t : t + 1] * total[t : t + 1]
+            im = im - sin_t[f, t : t + 1] * total[t : t + 1]
         amp.append((re * scale, im * scale))
     drive = []
     for t in range(STEPS):
         s = jnp.zeros((1, lanes), jnp.float32)
         for f in range(NF):
-            s = s + amp[f][0] * coef_ref[4 + f, t] + amp[f][1] * coef_ref[8 + f, t]
+            s = s + amp[f][0] * cos_t[f, t : t + 1] + amp[f][1] * sin_t[f, t : t + 1]
         drive.append(jnp.broadcast_to(s, (8, lanes)))
 
     for l in range(width):
@@ -448,8 +501,8 @@
                 for t in range(max(0, p - STEPS + 1), min(p, STEPS - 1) + 1):
                     term = first[t] * second[p - t]
                     q = term if q is None else q + term
-                perm = perm + coef_ref[0, p] * q
-                cond = cond + coef_ref[1, p] * q
+                perm = perm + corr[0, p + 1 : p + 2] * q
+                cond = cond + corr[1, p + 1 : p + 2] * q
             cells[c, l, pl.ds(b, 1)] = jnp.sum(perm, axis=0, keepdims=True)
             cells[3 + c, l, pl.ds(b, 1)] = jnp.sum(cond, axis=0, keepdims=True)
             return carry
@@ -469,7 +522,9 @@
     region = lax.broadcasted_iota(jnp.int32, (regions, lanes), 0)
     partial = jnp.zeros((8, regions), jnp.float32)
     for l in range(width):
-        hot = (region == jnp.broadcast_to(packed_ref[l : l + 1], (regions, lanes))).astype(
+        hot = (region == jnp.broadcast_to(
+                fact_own[1 + l : 2 + l].astype(jnp.int32), (regions, lanes)
+            )).astype(
             jnp.float32
         )
         these = jnp.concatenate([packed[:, l], jnp.zeros((2, lanes), jnp.float32)], axis=0)
@@ -488,7 +543,8 @@
     chosen = lax.broadcasted_iota(jnp.int32, (regions, lanes), 0)
     wanted = lax.broadcasted_iota(jnp.int32, (regions, lanes), 1) + me * per
     pick = ((chosen == wanted) & (wanted < (me + 1) * per)).astype(jnp.float32)
-    out_ref[...] = jnp.dot(summed, pick, precision=HIGH, preferred_element_type=jnp.float32)
+    mine = jnp.dot(summed, pick, precision=HIGH, preferred_element_type=jnp.float32)
+    out_ref[...] = mine[:6, :per]
 
     for r in range(2):
 
@@ -511,29 +567,6 @@
     rows, lanes = src_mode.shape
     per = perm.shape[1]
     regions = nd * per
-    me = lax.axis_index("domain")
-    both = jnp.concatenate([perm, cond, jnp.zeros((2, per), jnp.float32)], 0)
-    own = lax.div(jnp.arange(regions, dtype=jnp.int32), per) == me
-    tab = jnp.where(own[None], jnp.tile(both, (1, nd)), 0.0)
-    lab = jnp.repeat(labels, 8, axis=2)
-    packed = jnp.transpose(labels, (0, 2, 1)).reshape(width, lanes)
-    packed = jnp.concatenate([packed, jnp.zeros((-width % 8, lanes), jnp.int32)], 0)
-    omega = 0.25 + 0.05 * wave.astype(jnp.float32)
-    sums = jnp.arange(2, 2 * STEPS + 2).astype(jnp.float32)
-    angle = omega[:, None] * sums[None]
-    times = omega[:, None] * (jnp.arange(16).astype(jnp.float32) + 1.0)[None]
-    coef = jnp.concatenate(
-        [
-            jnp.sum((omega * omega)[:, None] * jnp.cos(angle), axis=0)[None],
-            -jnp.sum(omega[:, None] * jnp.sin(angle), axis=0)[None],
-            jnp.sum(jnp.sin(times), axis=0)[None],
-            jnp.zeros((1, 16), jnp.float32),
-            jnp.cos(times),
-            jnp.sin(times),
-        ],
-        0,
-    )
-    planes = jnp.concatenate([source, monitor])
     f32 = jnp.float32
     span = 2 * (STEPS - 1) + 1
     smem = pl.BlockSpec(memory_space=pltpu.SMEM)
@@ -543,8 +576,8 @@
     edge = pltpu.VMEM((2, STEPS, 2, rows, lanes), f32)
     out = pl.pallas_call(
         functools.partial(kernel, nd),
-        out_shape=jax.ShapeDtypeStruct((8, lanes), f32),
-        in_specs=[smem, smem, hbm, hbm, hbm, hbm, vmem, vmem, vmem, vmem, vmem],
+        out_shape=jax.ShapeDtypeStruct((6, per), f32),
+        in_specs=[smem, smem, smem, hbm, hbm, hbm, hbm, vmem, vmem, vmem, vmem, vmem],
         out_specs=vmem,
         scratch_shapes=[
             pltpu.VMEM((2, STEPS + 1, 3, width, rows, lanes), f32),
@@ -558,12 +591,16 @@
             pltpu.VMEM((STEPS, 3, span + 2, rows, lanes), f32),
             pltpu.VMEM((3, span + 2, rows, lanes), f32),
             pltpu.VMEM((6, span, rows, lanes), f32),
-            pltpu.VMEM((nd, 8, regions), f32),
-            pltpu.VMEM((nd, width, blocks, lanes), jnp.int32),
+            pltpu.VMEM((nd, 8, lanes), f32),
             pltpu.VMEM((nd, 16, lanes), f32),
             pltpu.VMEM((nd, 8, regions), f32),
             pltpu.VMEM((6, width, blocks, lanes), f32),
             pltpu.VMEM((8, regions), f32),
+            pltpu.VMEM((8, lanes), f32),
+            pltpu.VMEM((1 + width, 8, lanes), f32),
+            pltpu.VMEM((NF, 16, lanes), f32),
+            pltpu.VMEM((NF, 16, lanes), f32),
+            pltpu.VMEM((3, 16, lanes), f32),
             pltpu.VMEM((16, lanes), f32),
             pltpu.VMEM((8, regions), f32),
             dma((4,)),
@@ -571,14 +608,14 @@
             dma((2, STEPS)),
             dma((2, STEPS)),
             dma((2, STEPS)),
-            dma((4, nd)),
-            dma((4, nd)),
+            dma((3, nd)),
+            dma((3, nd)),
         ],
         compiler_params=pltpu.CompilerParams(
             collective_id=0, has_side_effects=True, vmem_limit_bytes=60 * 1024 * 1024
         ),
-    )(planes, coef, e, h, ae, ah, tab, lab, packed, src_mode, mon_mode)
-    return out[:6, :per]
+    )(source, monitor, wave, e, h, ae, ah, perm, cond, labels, src_mode, mon_mode)
+    return out
 
 
 def solution(mesh):

time: 70.5 us -> 59.1 us (0.84)
  Pallas kernels: 61.9 us -> 56.3 us
  local copies, waits for them, and re-layouts: 4.89 us -> 1.28 us
  other arithmetic: 2.09 us -> 0 us
    pallas_call x1, Pallas kernels: 61.9 us -> 56.3 us  [local(): pl.pallas_call(functools.partial(kernel, nd), out_shape=jax.ShapeDtypeStr...]
    concatenate x3 -> x0, local copies, waits for them, and re-layouts: 1.87 us -> none  [the longest x1 1.2 us: local(): jnp.concatenate([jnp.sum((omega * omega)[:, None] * jnp.cos(angle), axis=...]
    reshape x2 -> x0, local copies, waits for them, and re-layouts: 0.83 us -> none  [the longest x1 0.74 us: local(): lab = jnp.repeat(labels, 8, axis=2)]
    unnamed x7 -> x1, local copies, waits for them, and re-layouts: 1.88 us -> 1.28 us
where the time goes in v2:
time: 59.1 us; the launch traced here: 58.9 us
  Pallas kernels  56.3 us (95%)
  between operations  1.3 us (2%)
  local copies, waits for them, and re-layouts  1.28 us (2%)
    pallas_call x1, Pallas kernels, local(): pl.pallas_call(functools.partial(kernel, nd), out_shape=jax.ShapeDtypeStr...  56.3 us
    unnamed x1, local copies, waits for them, and re-layouts  1.28 us

profile of v2, /device:TPU:0, one launch (start us, length us, event | category | flops | bytes accessed | tf_op | source)
XLA Modules:
  0.0 58.9 jit_solution(12786331701493374024)
XLA Ops:
  1.3 56.3 %shard_map.118 = f32[6,8]{1,0:T(8,128)} custom-call(s32[1]{0:T(128)S(6)} %copy.14.source_ref, s32[1]{0:T(128)S(6)} %copy.15.monitor_ref, s32[4]{0:T(128)} %wave_ref.1, f32[3,4,64,128]{3,2,1,0:T(8,128)} %e_hbm.1, f32[3,4,64,128]{3,2,1,0:T(8,128)} %h_hbm.1, f32[3,4,64,128]{3,2,1,0:T(8,128)} %ae_hbm.1, f32[3,4,64,128]{3,2,1,0:T(8,128)} %ah_hbm.1, ...), custom_call_target="tpu_custom_call" | custom-call | tf_op jit(solution)/shard_map/pallas_call | solution.py:577
  57.6 1.3 %copy.16 = f32[6,8]{1,0:T(8,128)} copy(f32[6,8]{1,0:T(8,128)} %shard_map.118) | data formatting | bytes 384

commit v3 on v2

--- a/solution.py
+++ b/solution.py
@@ -405,6 +405,14 @@
 
         lax.fori_loop(reach + 1 - k, reach + 2 + k, one, 0)
 
+    mon_at = monitor - me * width
+    mon_ok = jnp.where((mon_at >= 0) & (mon_at < width), 1.0, 0.0)
+    mon_at = jnp.clip(mon_at, 0, width - 1)
+
+    def monitored(n):
+        prod = hist[0, n + 1, 1, mon_at] * mon_ref[...]
+        mid_own[pl.ds(n, 1)] = jnp.sum(prod, axis=0, keepdims=True) * mon_ok
+
     def step(n, carry):
         for r in range(2):
             electric_inner(r, n)
@@ -421,6 +429,7 @@
         for r in range(2):
             for l in range(1, last):
                 magnetic_inner(r, n, l)
+        monitored(n)
         return carry
 
     lax.fori_loop(0, STEPS - 1, step, 0)
@@ -429,15 +438,10 @@
     wait_right(0, n)
     electric_first(0, n)
 
-    mon_at = monitor - me * width
-    mon_ok = jnp.where((mon_at >= 0) & (mon_at < width), 1.0, 0.0)
-    mon_at = jnp.clip(mon_at, 0, width - 1)
     src_at = source - me * width
     src_ok = jnp.where((src_at >= 0) & (src_at < width), 1.0 / (rows * lanes), 0.0)
     src_at = jnp.clip(src_at, 0, width - 1)
-    for t in range(STEPS):
-        prod = hist[0, t + 1, 1, mon_at] * mon_ref[...]
-        mid_own[t : t + 1] = jnp.sum(prod, axis=0, keepdims=True) * mon_ok
+    monitored(n)
     for f in range(NF):
         re = jnp.zeros((rows, lanes), jnp.float32)
         im = jnp.zeros((rows, lanes), jnp.float32)
@@ -507,7 +511,7 @@
             cells[3 + c, l, pl.ds(b, 1)] = jnp.sum(cond, axis=0, keepdims=True)
             return carry
 
-        lax.fori_loop(0, 3 * blocks, correlate, 0)
+        lax.fori_loop(0, 3 * blocks, correlate, 0, unroll=2)
 
     left = lax.broadcasted_iota(jnp.int32, (lanes, lanes), 0)
     up = lax.broadcasted_iota(jnp.int32, (lanes, lanes), 1)

time: 59.1 us -> 58.1 us (0.983)
  Pallas kernels: 56.3 us -> 55.3 us
    pallas_call x1, Pallas kernels: 56.3 us -> 55.3 us  [local(): pl.pallas_call(functools.partial(kernel, nd), out_shape=jax.ShapeDtypeStr...]
where the time goes in v3:
time: 58.1 us; the launch traced here: 57.9 us
  Pallas kernels  55.3 us (95%)
  between operations  1.3 us (2%)
  local copies, waits for them, and re-layouts  1.28 us (2%)
    pallas_call x1, Pallas kernels, local(): pl.pallas_call(functools.partial(kernel, nd), out_shape=jax.ShapeDtypeStr...  55.3 us
    unnamed x1, local copies, waits for them, and re-layouts  1.28 us

profile of v3, /device:TPU:0, one launch (start us, length us, event | category | flops | bytes accessed | tf_op | source)
XLA Modules:
  0.0 57.9 jit_solution(4102286898009370988)
XLA Ops:
  1.3 55.3 %shard_map.118 = f32[6,8]{1,0:T(8,128)} custom-call(s32[1]{0:T(128)S(6)} %copy.14.source_ref, s32[1]{0:T(128)S(6)} %copy.15.monitor_ref, s32[4]{0:T(128)} %wave_ref.1, f32[3,4,64,128]{3,2,1,0:T(8,128)} %e_hbm.1, f32[3,4,64,128]{3,2,1,0:T(8,128)} %h_hbm.1, f32[3,4,64,128]{3,2,1,0:T(8,128)} %ae_hbm.1, f32[3,4,64,128]{3,2,1,0:T(8,128)} %ah_hbm.1, ...), custom_call_target="tpu_custom_call" | custom-call | tf_op jit(solution)/shard_map/pallas_call | solution.py:581
  56.6 1.3 %copy.16 = f32[6,8]{1,0:T(8,128)} copy(f32[6,8]{1,0:T(8,128)} %shard_map.118) | data formatting | bytes 384
